TPU v7x, 32 devices: a whole 2x2x4 slice. The times are simulated.
32 devices in a mesh: seq: 8 (over z, x), head: 4 (over y, core).
Axes of the slice: x: 2, y: 2, z: 4, core: 2. Of those that a mesh axis runs over, the one named last changes fastest.
Arguments:
- queries: bfloat16 [2, 8, 14336], P(None, 'seq', 'head'), may hold values from -150 to 150
- new_keys: bfloat16 [2, 8, 14336], P(None, 'seq', 'head'), may hold values from -6 to 6
- new_values: bfloat16 [2, 8, 14336], P(None, 'seq', 'head'), may hold values from -6 to 6
- cache_keys: bfloat16 [8192, 14336], P('seq', 'head'), may hold values from -6 to 6
- cache_values: bfloat16 [8192, 14336], P('seq', 'head'), may hold values from -6 to 6
- slopes: float32 [112], P('head'), may hold values from 7.324219e-05 to 0.025
- seg_blocks: int32 [8], replicated, may hold values from 1 to 32, 48 in all
- request_row: int32 [8], replicated, may hold values from 0 to 7, each once
- out_weight: bfloat16 [14336, 14336], P('head', 'seq'), may hold values from -0.046875 to 0.046875
- residual: bfloat16 [2, 8, 14336], P(None, 'head', 'seq'), may hold values from -6 to 6
Outputs:
- mixed: bfloat16 [2, 8, 14336], P(None, 'head', 'seq')
Inputs may be any that keep to these rules, and one draw needn't show every extreme that they name: `seg_blocks`: the requests are packed in order from block 0; 48 blocks are used and the rest of the cache is unused. `request_row`: each query row belongs to exactly one request.
All inputs are finite; a program needn't handle non-finite values.
Results may differ from a plain program's by a relative error of at most 0.006.
Values may be sent and summed in bfloat16 or wider, within the bound.
A program may use at most 64 MiB of HBM per device.

v0:
```python
import functools
import math

import jax
import jax.numpy as jnp
from jax import lax
from jax.experimental import pallas as pl
from jax.experimental.pallas import tpu as pltpu
from jax.sharding import PartitionSpec as P

BLK = 128
FAR = 1e35
LAG = 3
PARTS = 2
MESH = pl.DeviceIdType.MESH


def kernel(
    n_seq,
    n_head,
    heads,
    unit,
    tile,
    qry_ref,
    key_ref,
    val_ref,
    seg_ref,
    row_ref,
    slope_ref,
    res_ref,
    k_hbm,
    v_hbm,
    w_hbm,
    out_ref,
    kbuf,
    vbuf,
    wbuf,
    qall,
    own2d,
    qx,
    sbuf,
    pbuf,
    q2d,
    dist,
    o2d,
    st2d,
    sendb,
    recvb,
    attb,
    x_ref,
    sofar,
    shares,
    got,
    k_sem,
    v_sem,
    w_sem,
    q_send,
    q_recv,
    p_send,
    p_recv,
    a_send,
    a_recv,
    h_send,
    h_recv,
):
    hdim = qry_ref.shape[1] // heads
    rows = 2 * n_seq
    per = n_seq // n_head
    tokens = k_hbm.shape[0]
    padded = q2d.shape[0] // rows
    groups = heads // unit
    some = heads // PARTS
    slot = padded // PARTS
    wide = unit * hdim
    cols = w_hbm.shape[1]
    scale = 1.0 / math.sqrt(hdim)
    me = lax.axis_index("seq")
    mine = lax.axis_index("head")

    def k_copy(g):
        at = pl.ds(pl.multiple_of(g * wide, 128), wide)
        return pltpu.make_async_copy(k_hbm.at[:, at], kbuf.at[:, at], k_sem.at[g])

    def v_copy(g):
        at = pl.ds(pl.multiple_of(g * wide, 128), wide)
        return pltpu.make_async_copy(v_hbm.at[:, at], vbuf.at[:, at], v_sem.at[g])

    def w_copy(g):
        at = pl.ds(pl.multiple_of(g * wide, 128), wide)
        return pltpu.make_async_copy(w_hbm.at[at], wbuf.at[at], w_sem.at[g])

    def to_seq(step):
        return lax.rem(me + step, n_seq)

    def to_head(step):
        return lax.rem(mine + step, n_head)

    barrier = pltpu.get_barrier_semaphore()
    for step in range(1, n_seq):
        pl.semaphore_signal(
            barrier, inc=1, device_id={"seq": to_seq(step)}, device_id_type=MESH
        )
    for step in range(1, n_head):
        pl.semaphore_signal(
            barrier, inc=1, device_id={"head": to_head(step)}, device_id_type=MESH
        )
    for g in range(groups):
        k_copy(g).start()
        v_copy(g).start()
    for g in range(groups):
        w_copy(g).start()
    pl.semaphore_wait(barrier, n_seq + n_head - 2)

    def q_copy(step):
        return pltpu.make_async_remote_copy(
            src_ref=qry_ref,
            dst_ref=qall.at[me],
            send_sem=q_send.at[step - 1],
            recv_sem=q_recv.at[step - 1],
            device_id={"seq": to_seq(step)},
            device_id_type=MESH,
        )

    for step in range(1, n_seq):
        q_copy(step).start()

    line = lax.broadcasted_iota(jnp.int32, (rows, 1), 0)
    begin = jnp.zeros((rows, 1), jnp.int32)
    end = jnp.zeros((rows, 1), jnp.int32)
    at = jnp.int32(0)
    for i in range(n_seq):
        after = at + seg_ref[i]
        hit = (line // 2) == row_ref[i]
        begin = jnp.where(hit, at * BLK, begin)
        end = jnp.where(hit, after * BLK, end)
        at = after
    token = me * tokens + lax.broadcasted_iota(jnp.int32, (rows, tokens), 1)
    gap = (end + lax.rem(line, 2) - token).astype(jnp.float32)
    dist[...] = jnp.where((token >= begin) & (token < end), gap, FAR)

    lane = lax.broadcasted_iota(jnp.int32, (some, hdim), 1)
    hline = lax.broadcasted_iota(jnp.int32, (some, 1), 0)
    for n, ref in enumerate((qry_ref, key_ref, val_ref)):
        for h in range(heads):
            own2d[n, 2 * h : 2 * h + 2, :] = ref[:, h * hdim : (h + 1) * hdim].astype(jnp.float32)

    def own_terms(p):
        own = [
            [own2d.at[n][pl.ds(2 * p * some + t, some, stride=2), :] for t in range(2)]
            for n in range(3)
        ]
        slope_col = jnp.zeros((some, 1), jnp.float32)
        for h in range(some):
            slope_col = jnp.where(hline == h, slope_ref[p * some + h], slope_col)
        e00 = jnp.sum(own[0][0] * own[1][0], axis=-1, keepdims=True) * scale
        e10 = jnp.sum(own[0][1] * own[1][0], axis=-1, keepdims=True) * scale - slope_col
        e11 = jnp.sum(own[0][1] * own[1][1], axis=-1, keepdims=True) * scale
        upper = jnp.maximum(e10, e11)
        w10 = jnp.exp(e10 - upper)
        w11 = jnp.exp(e11 - upper)
        stat = jnp.where(
            lane == 0,
            e00,
            jnp.where(lane == 1, 1.0, jnp.where(lane == 2, upper, w10 + w11)),
        )
        return stat, [own[2][0], w10 * own[2][0] + w11 * own[2][1]]

    owned = [own_terms(p) for p in range(PARTS)]

    qall[me] = qry_ref[...]
    for step in range(1, n_seq):
        q_copy(step).wait_recv()
    for r in range(n_seq):
        qx[2 * r : 2 * r + 2, :] = qall[r].astype(jnp.float32)

    odd = lax.rem(lax.broadcasted_iota(jnp.int32, (rows, hdim), 1), 2) == 1

    def lanes(h):
        return slice(h * hdim, (h + 1) * hdim)

    def lines(h):
        return slice(h * rows, (h + 1) * rows)

    def scores(h):
        if h % unit == 0:
            k_copy(h // unit).wait()
        dots = lax.dot_general(
            qx[:, lanes(h)].astype(jnp.bfloat16),
            kbuf[:, lanes(h)],
            (((1,), (1,)), ((), ())),
            preferred_element_type=jnp.float32,
        )
        sbuf[lines(h), :] = dots * scale - slope_ref[h] * dist[...]

    def soften(h):
        score = sbuf[lines(h), :]
        top = jnp.max(score, axis=-1, keepdims=True)
        prob = jnp.exp(score - top)
        total = jnp.sum(prob, axis=-1, keepdims=True)
        pbuf[lines(h), :] = prob.astype(jnp.bfloat16)
        st2d[lines(h), :] = jnp.where(odd, total, top)

    def weigh(h):
        if h % unit == 0:
            v_copy(h // unit).wait()
        o2d[lines(h), :] = jnp.dot(
            pbuf[lines(h), :], vbuf[:, lanes(h)], preferred_element_type=jnp.float32
        )

    def message(p):
        base = p * some * rows
        for r in range(n_seq):
            first = st2d[pl.ds(base + 2 * r, some, stride=rows), :]
            second = st2d[pl.ds(base + 2 * r + 1, some, stride=rows), :]
            stat = jnp.where(lax.rem(lane, 4) < 2, first, second)
            high = stat.astype(jnp.bfloat16).astype(jnp.float32)
            rest = stat - high
            middle = rest.astype(jnp.bfloat16).astype(jnp.float32)
            low = rest - middle
            sendb[r, p, 2] = jnp.where(
                lane < 4, high, jnp.where(lane < 8, middle, low)
            ).astype(jnp.bfloat16)
            for s in range(2):
                sendb[r, p, s] = o2d[pl.ds(base + 2 * r + s, some, stride=rows), :].astype(
                    jnp.bfloat16
                )

    def p_copy(p, step):
        return pltpu.make_async_remote_copy(
            src_ref=sendb.at[to_seq(step), p],
            dst_ref=recvb.at[me, p],
            send_sem=p_send.at[p, step - 1],
            recv_sem=p_recv.at[p, step - 1],
            device_id={"seq": to_seq(step)},
            device_id_type=MESH,
        )

    for h in range(heads + 2 * LAG):
        if h < heads:
            scores(h)
        if 0 <= h - LAG < heads:
            soften(h - LAG)
        if 0 <= h - 2 * LAG:
            weigh(h - 2 * LAG)
        if h - 2 * LAG >= 0 and (h - 2 * LAG + 1) % some == 0:
            p = (h - 2 * LAG) // some
            message(p)
            for step in range(1, n_seq):
                p_copy(p, step).start()
            recvb[me, p] = sendb[me, p]

    pair = lax.div(me, per)
    place = lax.rem(me, per)

    def merge(p):
        own_stat, own_acc = owned[p]
        stats = [own_stat]
        for j in range(n_seq):
            x = recvb[j, p, 2].astype(jnp.float32)
            x = x + pltpu.roll(x, hdim - 4, 1) + pltpu.roll(x, hdim - 8, 1)
            stats.append(x)
        highest = functools.reduce(jnp.maximum, stats)
        factors = [jnp.exp(jnp.minimum(x - highest, 0.0)) for x in stats]
        total = sum(f * pltpu.roll(x, hdim - 1, 1) for f, x in zip(factors, stats))
        inverse = 1.0 / total
        for s in range(2):
            inv = inverse[:, 2 * s : 2 * s + 1]
            acc = factors[0][:, 2 * s : 2 * s + 1] * own_acc[s]
            for j in range(n_seq):
                acc += factors[j + 1][:, 2 * s : 2 * s + 1] * recvb[j, p, s].astype(jnp.float32)
            attb[pair, place, p, s] = (acc * inv).astype(jnp.bfloat16)

    def a_copy(p, step):
        return pltpu.make_async_remote_copy(
            src_ref=attb.at[pair, place, p],
            dst_ref=attb.at[pair, place, p],
            send_sem=a_send.at[p, step - 1],
            recv_sem=a_recv.at[p, step - 1],
            device_id={"seq": to_seq(step)},
            device_id_type=MESH,
        )

    def a_wait(p, step):
        source = lax.rem(me + n_seq - step, n_seq)
        here = attb.at[lax.div(source, per), lax.rem(source, per), p]
        return pltpu.make_async_remote_copy(
            src_ref=here,
            dst_ref=here,
            send_sem=a_send.at[p, step - 1],
            recv_sem=a_recv.at[p, step - 1],
            device_id={"seq": to_seq(step)},
            device_id_type=MESH,
        )

    for p in range(PARTS):
        for step in range(1, n_seq):
            p_copy(p, step).wait_recv()
        merge(p)
        for step in range(1, n_seq):
            a_copy(p, step).start()
    for g in range(groups):
        w_copy(g).wait()

    def h_copy(c, step):
        at = slice(c * tile, (c + 1) * tile)
        return pltpu.make_async_remote_copy(
            src_ref=shares.at[to_head(step), :, at],
            dst_ref=got.at[step - 1, :, at],
            send_sem=h_send.at[c, step - 1],
            recv_sem=h_recv.at[c, step - 1],
            device_id={"head": to_head(step)},
            device_id_type=MESH,
        )

    for p in range(PARTS):
        for step in range(1, n_seq):
            a_wait(p, step).wait_recv()
        for k in range(n_head):
            for s in range(2):
                for j in range(per):
                    n = (k * 2 + s) * per + j
                    q2d[pl.ds(n * padded + p * slot, some), :] = attb[k, j, p, s].astype(
                        jnp.float32
                    )
        for h in range(some):
            x_ref[:, lanes(p * some + h)] = q2d[
                pl.ds(p * slot + h, rows, stride=padded), :
            ].astype(jnp.bfloat16)
        deep = slice(p * some * hdim, (p + 1) * some * hdim)
        for c in range(cols // tile):
            at = slice(c * tile, (c + 1) * tile)
            part = jnp.dot(x_ref[:, deep], wbuf[deep, at], preferred_element_type=jnp.float32)
            if p > 0:
                part += sofar[:, at]
            if p < PARTS - 1:
                sofar[:, at] = part
                continue
            for k in range(n_head):
                shares[k, :, at] = part[2 * per * k : 2 * per * (k + 1)].astype(jnp.bfloat16)
            for step in range(1, n_head):
                h_copy(c, step).start()

    summed = shares[mine].astype(jnp.float32)
    for step in range(1, n_head):
        for c in range(cols // tile):
            h_copy(c, step).wait_recv()
        summed += got[step - 1].astype(jnp.float32)
    for s in range(2):
        out_ref[s] = (
            res_ref[s].astype(jnp.float32) + summed[s * per : (s + 1) * per]
        ).astype(jnp.bfloat16)
    for step in range(1, n_seq):
        q_copy(step).wait_send()
        for p in range(PARTS):
            p_copy(p, step).wait_send()
            a_copy(p, step).wait_send()
    for step in range(1, n_head):
        for c in range(cols // tile):
            h_copy(c, step).wait_send()


def body(
    n_seq,
    n_head,
    queries,
    new_keys,
    new_values,
    cache_keys,
    cache_values,
    slopes,
    seg_blocks,
    request_row,
    out_weight,
    residual,
):
    heads = slopes.shape[0]
    width = queries.shape[2]
    hdim = width // heads
    tokens = cache_keys.shape[0]
    cols = out_weight.shape[1]
    assert queries.shape[1] == 1 and seg_blocks.shape[0] == n_seq
    flat = [x.reshape(2, width) for x in (queries, new_keys, new_values)]
    unit = max(u for u in (1, 2, 4) if heads % u == 0)
    tile = 256 if cols % 256 == 0 else cols
    rows = 2 * n_seq
    per = n_seq // n_head
    some = heads // PARTS
    padded = PARTS * (-(-some // 8) * 8)
    assert heads % PARTS == 0
    groups = heads // unit
    bf16, f32 = jnp.bfloat16, jnp.float32
    dma = pltpu.SemaphoreType.DMA
    vmem = pl.BlockSpec(memory_space=pltpu.VMEM)
    smem = pl.BlockSpec(memory_space=pltpu.SMEM)
    hbm = pl.BlockSpec(memory_space=pl.ANY)
    return pl.pallas_call(
        functools.partial(kernel, n_seq, n_head, heads, unit, tile),
        out_shape=jax.ShapeDtypeStruct(residual.shape, residual.dtype),
        in_specs=[vmem, vmem, vmem, smem, smem, smem, vmem, hbm, hbm, hbm],
        out_specs=vmem,
        scratch_shapes=[
            pltpu.VMEM(cache_keys.shape, bf16),
            pltpu.VMEM(cache_values.shape, bf16),
            pltpu.VMEM(out_weight.shape, bf16),
            pltpu.VMEM((n_seq, 2, width), bf16),
            pltpu.VMEM((3, 2 * heads, hdim), f32),
            pltpu.VMEM((rows, width), f32),
            pltpu.VMEM((heads * rows, tokens), f32),
            pltpu.VMEM((heads * rows, tokens), bf16),
            pltpu.VMEM((rows * padded, hdim), f32),
            pltpu.VMEM((rows, tokens), f32),
            pltpu.VMEM((heads * rows, hdim), f32),
            pltpu.VMEM((heads * rows, hdim), f32),
            pltpu.VMEM((n_seq, PARTS, 3, some, hdim), bf16),
            pltpu.VMEM((n_seq, PARTS, 3, some, hdim), bf16),
            pltpu.VMEM((n_head, per, PARTS, 2, some, hdim), bf16),
            pltpu.VMEM((rows, width), bf16),
            pltpu.VMEM((rows, cols), f32),
            pltpu.VMEM((n_head, 2 * per, cols), bf16),
            pltpu.VMEM((n_head - 1, 2 * per, cols), bf16),
            dma((groups,)),
            dma((groups,)),
            dma((groups,)),
            dma((n_seq - 1,)),
            dma((n_seq - 1,)),
            dma((PARTS, n_seq - 1)),
            dma((PARTS, n_seq - 1)),
            dma((PARTS, n_seq - 1)),
            dma((PARTS, n_seq - 1)),
            dma((cols // tile, n_head - 1)),
            dma((cols // tile, n_head - 1)),
        ],
        compiler_params=pltpu.CompilerParams(
            collective_id=0, has_side_effects=True, vmem_limit_bytes=56 << 20
        ),
    )(*flat, seg_blocks, request_row, slopes, residual, cache_keys, cache_values, out_weight)


def solution(mesh):
    in_specs = (
        P(None, "seq", "head"),
        P(None, "seq", "head"),
        P(None, "seq", "head"),
        P("seq", "head"),
        P("seq", "head"),
        P("head"),
        P(),
        P(),
        P("head", "seq"),
        P(None, "head", "seq"),
    )
    out_specs = P(None, "head", "seq")
    sizes = (mesh.shape["seq"], mesh.shape["head"])
    return jax.shard_map(
        functools.partial(body, *sizes),
        mesh=mesh,
        in_specs=in_specs,
        out_specs=out_specs,
        check_vma=False,
    )
```

profile of v0, /device:TPU:0, one launch (start us, length us, event | category | flops | bytes accessed | tf_op | source)
XLA Modules:
  0.0 33.2 jit_solution(2507496045471173926)
XLA Ops:
  0.0 31.9 %shard_map.100 = bf16[2,2,1792]{2,1,0:T(2,128)(2,1)} custom-call(bf16[2,3584]{1,0:T(2,128)(2,1)} %bitcast.3, bf16[2,3584]{1,0:T(2,128)(2,1)} %bitcast.4, bf16[2,3584]{1,0:T(2,128)(2,1)} %bitcast.5, s32[8]{0:T(128)} %seg_ref.1, s32[8]{0:T(128)} %row_ref.1, f32[28]{0:T(128)} %slope_ref.1, bf16[2,2,1792]{2,1,0:T(2,128)(2,1)} %res_ref.1, ...), custom_call_target="tpu_custom_call" | custom-call | tf_op jit(solution)/shard_map/pallas_call | solution.py:396
  31.9 1.3 %copy.12 = bf16[2,2,1792]{2,1,0:T(2,128)(2,1)} copy(bf16[2,2,1792]{2,1,0:T(2,128)(2,1)} %shard_map.100) | data formatting | bytes 28672
where the time goes:
time: 33.6 us; the launch traced here: 33.2 us
  Pallas kernels  31.9 us (95%)
  local copies, waits for them, and re-layouts  1.32 us (4%)
    pallas_call x1, Pallas kernels, body(): pl.pallas_call(functools.partial(kernel, n_seq, n_head, heads, unit, tile...  31.9 us
    unnamed x1, local copies, waits for them, and re-layouts  1.32 us

commit v1 on v0

v1 whole, which is shorter than its diff:
```python
import functools
import math

import jax
import jax.numpy as jnp
from jax import lax
from jax.experimental import pallas as pl
from jax.experimental.pallas import tpu as pltpu
from jax.sharding import PartitionSpec as P

BLK = 128
FAR = 1e35
LAG = 3
PARTS = 2
MESH = pl.DeviceIdType.MESH


def kernel(
    n_seq,
    n_head,
    heads,
    unit,
    tile,
    live,
    first,
    mergers,
    qry_ref,
    key_ref,
    val_ref,
    seg_ref,
    row_ref,
    slope_ref,
    res_ref,
    k_hbm,
    v_hbm,
    w_hbm,
    out_ref,
    kbuf,
    vbuf,
    wbuf,
    qall,
    kvown,
    own2d,
    qx,
    sbuf,
    pbuf,
    q2d,
    dist,
    o2d,
    st2d,
    sendb,
    recvb,
    xin,
    sofar,
    shares,
    got,
    k_sem,
    v_sem,
    w_sem,
    q_send,
    q_recv,
    kv_send,
    kv_recv,
    p_send,
    p_recv,
    a_send,
    a_recv,
    h_send,
    h_recv,
):
    hdim = qry_ref.shape[1] // heads
    rows = 2 * n_seq
    per = n_seq // n_head
    owned = n_seq // mergers
    tokens = k_hbm.shape[0]
    groups = heads // unit
    some = heads // PARTS
    slot = q2d.shape[0] // (2 * owned)
    wide = unit * hdim
    cols = w_hbm.shape[1]
    scale = 1.0 / math.sqrt(hdim)
    me = lax.axis_index("seq")
    mine = lax.axis_index("head")
    is_live = me < live
    is_merger = (me >= first) & (me < first + mergers)

    def k_copy(g):
        at = pl.ds(pl.multiple_of(g * wide, 128), wide)
        return pltpu.make_async_copy(k_hbm.at[:, at], kbuf.at[:, at], k_sem.at[g])

    def v_copy(g):
        at = pl.ds(pl.multiple_of(g * wide, 128), wide)
        return pltpu.make_async_copy(v_hbm.at[:, at], vbuf.at[:, at], v_sem.at[g])

    def w_copy(g):
        at = pl.ds(pl.multiple_of(g * wide, 128), wide)
        return pltpu.make_async_copy(w_hbm.at[at], wbuf.at[at], w_sem.at[g])

    def to_seq(step):
        return lax.rem(me + step, n_seq)

    def to_live(step):
        return lax.rem(me + step, live)

    def to_head(step):
        return lax.rem(mine + step, n_head)

    def remote(src, dst, send, recv, axis, to):
        return pltpu.make_async_remote_copy(
            src_ref=src,
            dst_ref=dst,
            send_sem=send,
            recv_sem=recv,
            device_id={axis: to},
            device_id_type=MESH,
        )

    barrier = pltpu.get_barrier_semaphore()

    @pl.when(is_live)
    def _():
        for step in range(1, n_seq):
            pl.semaphore_signal(
                barrier, inc=1, device_id={"seq": to_seq(step)}, device_id_type=MESH
            )

    for step in range(1, n_head):
        pl.semaphore_signal(
            barrier, inc=1, device_id={"head": to_head(step)}, device_id_type=MESH
        )

    @pl.when(is_live)
    def _():
        for g in range(groups):
            k_copy(g).start()
            v_copy(g).start()

    for g in range(groups):
        w_copy(g).start()

    def q_copy(n, to):
        return remote(qry_ref, qall.at[me], q_send.at[n], q_recv.at[me], "seq", to)

    @pl.when(is_live)
    def _():
        pl.semaphore_wait(barrier, live - 1 + n_head - 1)
        for step in range(1, live):
            q_copy(step - 1, to_live(step)).start()

    @pl.when(jnp.logical_not(is_live))
    def _():
        pl.semaphore_wait(barrier, live + n_head - 1)
        for d in range(live):
            q_copy(d, d).start()

    keeper = first + lax.div(me, owned)
    place = lax.rem(me, owned)

    def kv_copy(n, slot):
        ref = (key_ref, val_ref)[n]
        return remote(
            ref, kvown.at[slot, n], kv_send.at[n], kv_recv.at[slot, n], "seq", keeper
        )

    @pl.when(keeper != me)
    def _():
        for n in range(2):
            kv_copy(n, place).start()

    @pl.when(keeper == me)
    def _():
        kvown[place, 0] = key_ref[...]
        kvown[place, 1] = val_ref[...]

    lane = lax.broadcasted_iota(jnp.int32, (some, hdim), 1)
    hline = lax.broadcasted_iota(jnp.int32, (some, 1), 0)

    def lanes(h):
        return slice(h * hdim, (h + 1) * hdim)

    def lines(h):
        return slice(h * rows, (h + 1) * rows)

    def p_copy(p, m):
        return remote(
            sendb.at[m, p], recvb.at[me, p], p_send.at[p, m], p_recv.at[p, me], "seq", first + m
        )

    @pl.when(is_live)
    def attend():
        line = lax.broadcasted_iota(jnp.int32, (rows, 1), 0)
        begin = jnp.zeros((rows, 1), jnp.int32)
        end = jnp.zeros((rows, 1), jnp.int32)
        at = jnp.int32(0)
        for i in range(n_seq):
            after = at + seg_ref[i]
            hit = (line // 2) == row_ref[i]
            begin = jnp.where(hit, at * BLK, begin)
            end = jnp.where(hit, after * BLK, end)
            at = after
        token = me * tokens + lax.broadcasted_iota(jnp.int32, (rows, tokens), 1)
        gap = (end + lax.rem(line, 2) - token).astype(jnp.float32)
        dist[...] = jnp.where((token >= begin) & (token < end), gap, FAR)
        odd = lax.rem(lax.broadcasted_iota(jnp.int32, (rows, hdim), 1), 2) == 1

        for g in range(groups):
            k_copy(g).wait()
            v_copy(g).wait()
        qall[me] = qry_ref[...]
        for step in range(1, n_seq):
            source = to_seq(step)
            remote(
                qry_ref, qall.at[source], q_send.at[0], q_recv.at[source], "seq", source
            ).wait_recv()
        for r in range(n_seq):
            qx[2 * r : 2 * r + 2, :] = qall[r].astype(jnp.float32)

        def scores(h):
            dots = lax.dot_general(
                qx[:, lanes(h)].astype(jnp.bfloat16),
                kbuf[:, lanes(h)],
                (((1,), (1,)), ((), ())),
                preferred_element_type=jnp.float32,
            )
            sbuf[lines(h), :] = dots * scale - slope_ref[h] * dist[...]

        def soften(h):
            score = sbuf[lines(h), :]
            top = jnp.max(score, axis=-1, keepdims=True)
            prob = jnp.exp(score - top)
            total = jnp.sum(prob, axis=-1, keepdims=True)
            pbuf[lines(h), :] = prob.astype(jnp.bfloat16)
            st2d[lines(h), :] = jnp.where(odd, total, top)

        def weigh(h):
            o2d[lines(h), :] = jnp.dot(
                pbuf[lines(h), :], vbuf[:, lanes(h)], preferred_element_type=jnp.float32
            )

        def message(p):
            base = p * some * rows
            for m in range(mergers):
                stat = None
                for k in range(owned):
                    for s in range(2):
                        n = 2 * (m * owned + k) + s
                        x = st2d[pl.ds(base + n, some, stride=rows), :]
                        here = (lane // 16 == k) & (lax.rem(lane, 4) // 2 == s)
                        stat = x if stat is None else jnp.where(here, x, stat)
                        sendb[m, p, 2 * k + s] = o2d[
                            pl.ds(base + n, some, stride=rows), :
                        ].astype(jnp.bfloat16)
                high = stat.astype(jnp.bfloat16).astype(jnp.float32)
                rest = stat - high
                middle = rest.astype(jnp.bfloat16).astype(jnp.float32)
                low = rest - middle
                piece = lax.rem(lane, 16) // 4
                sendb[m, p, 2 * owned] = jnp.where(
                    piece == 0, high, jnp.where(piece == 1, middle, low)
                ).astype(jnp.bfloat16)

        for h in range(heads + 2 * LAG):
            if h < heads:
                scores(h)
            if 0 <= h - LAG < heads:
                soften(h - LAG)
            if 0 <= h - 2 * LAG:
                weigh(h - 2 * LAG)
            if h - 2 * LAG >= 0 and (h - 2 * LAG + 1) % some == 0:
                p = (h - 2 * LAG) // some
                message(p)
                for m in range(mergers):

                    @pl.when(me != first + m)
                    def _():
                        p_copy(p, m).start()

                    @pl.when(me == first + m)
                    def _():
                        recvb[me, p] = sendb[m, p]

    group = me - first

    def a_copy(p, to, n):
        return remote(
            xin.at[group, p], xin.at[group, p], a_send.at[p, n], a_recv.at[p, group], "seq", to
        )

    @pl.when(is_merger)
    def combine():
        base = group * owned
        for k in range(owned):

            @pl.when(base + k != me)
            def _():
                for n in range(2):
                    kv_copy(n, k).wait_recv()

        for k in range(owned):
            parts = (qall.at[base + k], kvown.at[k, 0], kvown.at[k, 1])
            for n, ref in enumerate(parts):
                for h in range(heads):
                    own2d[k, n, 2 * h : 2 * h + 2, :] = ref[:, lanes(h)].astype(jnp.float32)

        def own_terms(k, p):
            own = [
                [own2d.at[k, n][pl.ds(2 * p * some + t, some, stride=2), :] for t in range(2)]
                for n in range(3)
            ]
            slope_col = jnp.zeros((some, 1), jnp.float32)
            for h in range(some):
                slope_col = jnp.where(hline == h, slope_ref[p * some + h], slope_col)
            e00 = jnp.sum(own[0][0] * own[1][0], axis=-1, keepdims=True) * scale
            e10 = jnp.sum(own[0][1] * own[1][0], axis=-1, keepdims=True) * scale - slope_col
            e11 = jnp.sum(own[0][1] * own[1][1], axis=-1, keepdims=True) * scale
            upper = jnp.maximum(e10, e11)
            w10 = jnp.exp(e10 - upper)
            w11 = jnp.exp(e11 - upper)
            j = lax.rem(lane, 4)
            stat = jnp.where(
                j == 0, e00, jnp.where(j == 1, 1.0, jnp.where(j == 2, upper, w10 + w11))
            )
            return stat, [own[2][0], w10 * own[2][0] + w11 * own[2][1]]

        own = [[own_terms(k, p) for k in range(owned)] for p in range(PARTS)]

        def merge(p):
            stat = own[p][0][0]
            for k in range(1, owned):
                stat = jnp.where(lane // 16 == k, own[p][k][0], stat)
            stats = [stat]
            for j in range(live):
                x = recvb[j, p, 2 * owned].astype(jnp.float32)
                x = x + pltpu.roll(x, hdim - 4, 1) + pltpu.roll(x, hdim - 8, 1)
                stats.append(x)
            highest = functools.reduce(jnp.maximum, stats)
            factors = [jnp.exp(jnp.minimum(x - highest, 0.0)) for x in stats]
            total = sum(f * pltpu.roll(x, hdim - 1, 1) for f, x in zip(factors, stats))
            inverse = 1.0 / total
            for k in range(owned):
                for s in range(2):
                    c = slice(16 * k + 2 * s, 16 * k + 2 * s + 1)
                    acc = factors[0][:, c] * own[p][k][1][s]
                    for j in range(live):
                        acc += factors[j + 1][:, c] * recvb[j, p, 2 * k + s].astype(jnp.float32)
                    n = k // per * 2 * per + s * per + k % per
                    q2d[pl.ds(n * slot, some), :] = acc * inverse[:, c]
            for h in range(some):
                xin[group, p, :, lanes(h)] = q2d[
                    pl.ds(h, 2 * owned, stride=slot), :
                ].astype(jnp.bfloat16)

        for p in range(PARTS):
            for step in range(1, live):
                source = to_live(step)
                remote(
                    sendb.at[0, p], recvb.at[source, p], p_send.at[p, 0], p_recv.at[p, source],
                    "seq", source,
                ).wait_recv()
            merge(p)
            for n in range(1, n_seq):
                a_copy(p, to_seq(n_seq - n), n - 1).start()

    for g in range(groups):
        w_copy(g).wait()

    def h_copy(c, step):
        at = slice(c * tile, (c + 1) * tile)
        return remote(
            shares.at[to_head(step), :, at],
            got.at[step - 1, :, at],
            h_send.at[c, step - 1],
            h_recv.at[c, step - 1],
            "head",
            to_head(step),
        )

    for p in range(PARTS):
        for m in range(mergers):

            @pl.when(me != first + m)
            def _():
                here = xin.at[m, p]
                remote(
                    here, here, a_send.at[p, 0], a_recv.at[p, m], "seq", first + m
                ).wait_recv()

        x = jnp.concatenate([xin[m, p] for m in range(mergers)], axis=0)
        deep = slice(p * some * hdim, (p + 1) * some * hdim)
        for c in range(cols // tile):
            at = slice(c * tile, (c + 1) * tile)
            part = jnp.dot(x, wbuf[deep, at], preferred_element_type=jnp.float32)
            if p > 0:
                part += sofar[:, at]
            if p < PARTS - 1:
                sofar[:, at] = part
                continue
            for k in range(n_head):
                shares[k, :, at] = part[2 * per * k : 2 * per * (k + 1)].astype(jnp.bfloat16)
            for step in range(1, n_head):
                h_copy(c, step).start()

    summed = shares[mine].astype(jnp.float32)
    for step in range(1, n_head):
        for c in range(cols // tile):
            h_copy(c, step).wait_recv()
        summed += got[step - 1].astype(jnp.float32)
    for s in range(2):
        out_ref[s] = (
            res_ref[s].astype(jnp.float32) + summed[s * per : (s + 1) * per]
        ).astype(jnp.bfloat16)

    @pl.when(is_live)
    def _():
        for step in range(1, live):
            q_copy(step - 1, to_live(step)).wait_send()
        for m in range(mergers):

            @pl.when(me != first + m)
            def _():
                for p in range(PARTS):
                    p_copy(p, m).wait_send()

    @pl.when(jnp.logical_not(is_live))
    def _():
        for d in range(live):
            q_copy(d, d).wait_send()

    @pl.when(keeper != me)
    def _():
        for n in range(2):
            kv_copy(n, place).wait_send()

    @pl.when(is_merger)
    def _():
        for p in range(PARTS):
            for n in range(1, n_seq):
                a_copy(p, to_seq(n_seq - n), n - 1).wait_send()

    for step in range(1, n_head):
        for c in range(cols // tile):
            h_copy(c, step).wait_send()


def body(
    n_seq,
    n_head,
    queries,
    new_keys,
    new_values,
    cache_keys,
    cache_values,
    slopes,
    seg_blocks,
    request_row,
    out_weight,
    residual,
):
    heads = slopes.shape[0]
    width = queries.shape[2]
    hdim = width // heads
    tokens = cache_keys.shape[0]
    cols = out_weight.shape[1]
    assert queries.shape[1] == 1 and seg_blocks.shape[0] == n_seq
    flat = [x.reshape(2, width) for x in (queries, new_keys, new_values)]
    unit = max(u for u in (1, 2, 4) if heads % u == 0)
    tile = 256 if cols % 256 == 0 else cols
    rows = 2 * n_seq
    per = n_seq // n_head
    some = heads // PARTS
    slot = -(-some // 8) * 8
    live, first, mergers = 3 * n_seq // 4, n_seq // 4, n_seq // 4
    owned = n_seq // mergers
    assert n_seq % 4 == 0 and owned % per == 0 and 16 * owned <= hdim
    assert heads % PARTS == 0
    groups = heads // unit
    bf16, f32 = jnp.bfloat16, jnp.float32
    dma = pltpu.SemaphoreType.DMA
    vmem = pl.BlockSpec(memory_space=pltpu.VMEM)
    smem = pl.BlockSpec(memory_space=pltpu.SMEM)
    hbm = pl.BlockSpec(memory_space=pl.ANY)
    return pl.pallas_call(
        functools.partial(kernel, n_seq, n_head, heads, unit, tile, live, first, mergers),
        out_shape=jax.ShapeDtypeStruct(residual.shape, residual.dtype),
        in_specs=[vmem, vmem, vmem, smem, smem, smem, vmem, hbm, hbm, hbm],
        out_specs=vmem,
        scratch_shapes=[
            pltpu.VMEM(cache_keys.shape, bf16),
            pltpu.VMEM(cache_values.shape, bf16),
            pltpu.VMEM(out_weight.shape, bf16),
            pltpu.VMEM((n_seq, 2, width), bf16),
            pltpu.VMEM((owned, 2, 2, width), bf16),
            pltpu.VMEM((owned, 3, 2 * heads, hdim), f32),
            pltpu.VMEM((rows, width), f32),
            pltpu.VMEM((heads * rows, tokens), f32),
            pltpu.VMEM((heads * rows, tokens), bf16),
            pltpu.VMEM((2 * owned * slot, hdim), f32),
            pltpu.VMEM((rows, tokens), f32),
            pltpu.VMEM((heads * rows, hdim), f32),
            pltpu.VMEM((heads * rows, hdim), f32),
            pltpu.VMEM((mergers, PARTS, 2 * owned + 1, some, hdim), bf16),
            pltpu.VMEM((live, PARTS, 2 * owned + 1, some, hdim), bf16),
            pltpu.VMEM((mergers, PARTS, 2 * owned, some * hdim), bf16),
            pltpu.VMEM((rows, cols), f32),
            pltpu.VMEM((n_head, 2 * per, cols), bf16),
            pltpu.VMEM((n_head - 1, 2 * per, cols), bf16),
            dma((groups,)),
            dma((groups,)),
            dma((groups,)),
            dma((live,)),
            dma((n_seq,)),
            dma((2,)),
            dma((owned, 2)),
            dma((PARTS, mergers)),
            dma((PARTS, live)),
            dma((PARTS, n_seq - 1)),
            dma((PARTS, mergers)),
            dma((cols // tile, n_head - 1)),
            dma((cols // tile, n_head - 1)),
        ],
        compiler_params=pltpu.CompilerParams(
            collective_id=0, has_side_effects=True, vmem_limit_bytes=56 << 20
        ),
    )(*flat, seg_blocks, request_row, slopes, residual, cache_keys, cache_values, out_weight)


def solution(mesh):
    in_specs = (
        P(None, "seq", "head"),
        P(None, "seq", "head"),
        P(None, "seq", "head"),
        P("seq", "head"),
        P("seq", "head"),
        P("head"),
        P(),
        P(),
        P("head", "seq"),
        P(None, "head", "seq"),
    )
    out_specs = P(None, "head", "seq")
    sizes = (mesh.shape["seq"], mesh.shape["head"])
    return jax.shard_map(
        functools.partial(body, *sizes),
        mesh=mesh,
        in_specs=in_specs,
        out_specs=out_specs,
        check_vma=False,
    )
```

time: 33.6 us -> 33.4 us (level)
  no operation moved by 1% of the time
where the time goes in v1:
time: 33.4 us; the launch traced here: 33.1 us
  Pallas kernels  31.8 us (95%)
  local copies, waits for them, and re-layouts  1.32 us (4%)
    pallas_call x1, Pallas kernels, body(): pl.pallas_call(functools.partial(kernel, n_seq, n_head, heads, unit, tile...  31.8 us
    unnamed x1, local copies, waits for them, and re-layouts  1.32 us

profile of v1, /device:TPU:0, one launch (start us, length us, event | category | flops | bytes accessed | tf_op | source)
XLA Modules:
  0.0 33.1 jit_solution(16987093718399839157)
XLA Ops:
  0.0 31.8 %shard_map.100 = bf16[2,2,1792]{2,1,0:T(2,128)(2,1)} custom-call(bf16[2,3584]{1,0:T(2,128)(2,1)} %bitcast.3, bf16[2,3584]{1,0:T(2,128)(2,1)} %bitcast.4, bf16[2,3584]{1,0:T(2,128)(2,1)} %bitcast.5, s32[8]{0:T(128)} %seg_ref.1, s32[8]{0:T(128)} %row_ref.1, f32[28]{0:T(128)} %slope_ref.1, bf16[2,2,1792]{2,1,0:T(2,128)(2,1)} %res_ref.1, ...), custom_call_target="tpu_custom_call" | custom-call | tf_op jit(solution)/shard_map/pallas_call | solution.py:482
  31.8 1.3 %copy.12 = bf16[2,2,1792]{2,1,0:T(2,128)(2,1)} copy(bf16[2,2,1792]{2,1,0:T(2,128)(2,1)} %shard_map.100) | data formatting | bytes 28672

commit v2 on v1

--- a/solution.py
+++ b/solution.py
@@ -115,6 +115,17 @@
             device_id_type=MESH,
         )
 
+    @pl.when(is_live)
+    def _():
+        for g in range(groups):
+            k_copy(g).start()
+            v_copy(g).start()
+
+    @pl.when(jnp.logical_not(is_live))
+    def _():
+        for g in range(groups):
+            w_copy(g).start()
+
     barrier = pltpu.get_barrier_semaphore()
 
     @pl.when(is_live)
@@ -128,15 +139,6 @@
         pl.semaphore_signal(
             barrier, inc=1, device_id={"head": to_head(step)}, device_id_type=MESH
         )
-
-    @pl.when(is_live)
-    def _():
-        for g in range(groups):
-            k_copy(g).start()
-            v_copy(g).start()
-
-    for g in range(groups):
-        w_copy(g).start()
 
     def q_copy(n, to):
         return remote(qry_ref, qall.at[me], q_send.at[n], q_recv.at[me], "seq", to)
@@ -203,9 +205,6 @@
         dist[...] = jnp.where((token >= begin) & (token < end), gap, FAR)
         odd = lax.rem(lax.broadcasted_iota(jnp.int32, (rows, hdim), 1), 2) == 1
 
-        for g in range(groups):
-            k_copy(g).wait()
-            v_copy(g).wait()
         qall[me] = qry_ref[...]
         for step in range(1, n_seq):
             source = to_seq(step)
@@ -260,6 +259,13 @@
                 ).astype(jnp.bfloat16)
 
         for h in range(heads + 2 * LAG):
+            if h % some == 0 and h < heads:
+                for g in range(h // unit, (h + some) // unit):
+                    k_copy(g).wait()
+                    v_copy(g).wait()
+                if h + some == heads:
+                    for g in range(groups):
+                        w_copy(g).start()
             if h < heads:
                 scores(h)
             if 0 <= h - LAG < heads:
@@ -463,8 +469,8 @@
     cols = out_weight.shape[1]
     assert queries.shape[1] == 1 and seg_blocks.shape[0] == n_seq
     flat = [x.reshape(2, width) for x in (queries, new_keys, new_values)]
-    unit = max(u for u in (1, 2, 4) if heads % u == 0)
-    tile = 256 if cols % 256 == 0 else cols
+    unit = heads // 2
+    tile = cols
     rows = 2 * n_seq
     per = n_seq // n_head
     some = heads // PARTS

time: 33.4 us -> 29.6 us (0.89)
  Pallas kernels: 31.8 us -> 28 us
    pallas_call x1, Pallas kernels: 31.8 us -> 28 us  [body(): pl.pallas_call(functools.partial(kernel, n_seq, n_head, heads, unit, tile...]
where the time goes in v2:
time: 29.6 us; the launch traced here: 29.3 us
  Pallas kernels  28 us (95%)
  local copies, waits for them, and re-layouts  1.32 us (4%)
    pallas_call x1, Pallas kernels, body(): pl.pallas_call(functools.partial(kernel, n_seq, n_head, heads, unit, tile...  28 us
    unnamed x1, local copies, waits for them, and re-layouts  1.32 us

profile of v2, /device:TPU:0, one launch (start us, length us, event | category | flops | bytes accessed | tf_op | source)
XLA Modules:
  0.0 29.3 jit_solution(6328192550064050021)
XLA Ops:
  0.0 28.0 %shard_map.100 = bf16[2,2,1792]{2,1,0:T(2,128)(2,1)} custom-call(bf16[2,3584]{1,0:T(2,128)(2,1)} %bitcast.3, bf16[2,3584]{1,0:T(2,128)(2,1)} %bitcast.4, bf16[2,3584]{1,0:T(2,128)(2,1)} %bitcast.5, s32[8]{0:T(128)} %seg_ref.1, s32[8]{0:T(128)} %row_ref.1, f32[28]{0:T(128)} %slope_ref.1, bf16[2,2,1792]{2,1,0:T(2,128)(2,1)} %res_ref.1, ...), custom_call_target="tpu_custom_call" | custom-call | tf_op jit(solution)/shard_map/pallas_call | solution.py:488
  28.0 1.3 %copy.12 = bf16[2,2,1792]{2,1,0:T(2,128)(2,1)} copy(bf16[2,2,1792]{2,1,0:T(2,128)(2,1)} %shard_map.100) | data formatting | bytes 28672

commit v3 on v2

--- a/solution.py
+++ b/solution.py
@@ -11,7 +11,6 @@
 BLK = 128
 FAR = 1e35
 LAG = 3
-PARTS = 2
 MESH = pl.DeviceIdType.MESH
 
 
@@ -24,6 +23,18 @@
     live,
     first,
     mergers,
+    sizes,
+    qry_hbm,
+    key_hbm,
+    val_hbm,
+    seg_hbm,
+    row_hbm,
+    slope_hbm,
+    res_hbm,
+    k_hbm,
+    v_hbm,
+    w_hbm,
+    out_ref,
     qry_ref,
     key_ref,
     val_ref,
@@ -31,10 +42,7 @@
     row_ref,
     slope_ref,
     res_ref,
-    k_hbm,
-    v_hbm,
-    w_hbm,
-    out_ref,
+    i_sem,
     kbuf,
     vbuf,
     wbuf,
@@ -74,7 +82,8 @@
     owned = n_seq // mergers
     tokens = k_hbm.shape[0]
     groups = heads // unit
-    some = heads // PARTS
+    parts = len(sizes)
+    starts = [sum(sizes[:p]) for p in range(parts)]
     slot = q2d.shape[0] // (2 * owned)
     wide = unit * hdim
     cols = w_hbm.shape[1]
@@ -96,11 +105,29 @@
         at = pl.ds(pl.multiple_of(g * wide, 128), wide)
         return pltpu.make_async_copy(w_hbm.at[at], wbuf.at[at], w_sem.at[g])
 
+    staged = [
+        pltpu.make_async_copy(src, dst, i_sem.at[n])
+        for n, (src, dst) in enumerate(
+            (
+                (qry_hbm, qry_ref),
+                (key_hbm, key_ref),
+                (val_hbm, val_ref),
+                (seg_hbm, seg_ref),
+                (row_hbm, row_ref),
+                (slope_hbm, slope_ref),
+                (res_hbm, res_ref),
+            )
+        )
+    ]
+
     def to_seq(step):
         return lax.rem(me + step, n_seq)
 
     def to_live(step):
         return lax.rem(me + step, live)
+
+    def other(n):
+        return n + jnp.where(me <= n, 1, 0)
 
     def to_head(step):
         return lax.rem(mine + step, n_head)
@@ -121,11 +148,6 @@
             k_copy(g).start()
             v_copy(g).start()
 
-    @pl.when(jnp.logical_not(is_live))
-    def _():
-        for g in range(groups):
-            w_copy(g).start()
-
     barrier = pltpu.get_barrier_semaphore()
 
     @pl.when(is_live)
@@ -140,8 +162,11 @@
             barrier, inc=1, device_id={"head": to_head(step)}, device_id_type=MESH
         )
 
+    for copy in staged:
+        copy.start()
+
     def q_copy(n, to):
-        return remote(qry_ref, qall.at[me], q_send.at[n], q_recv.at[me], "seq", to)
+        return remote(qry_hbm, qall.at[me], q_send.at[n], q_recv.at[me], "seq", to)
 
     @pl.when(is_live)
     def _():
@@ -154,12 +179,14 @@
         pl.semaphore_wait(barrier, live + n_head - 1)
         for d in range(live):
             q_copy(d, d).start()
+        for g in range(groups):
+            w_copy(g).start()
 
     keeper = first + lax.div(me, owned)
     place = lax.rem(me, owned)
 
     def kv_copy(n, slot):
-        ref = (key_ref, val_ref)[n]
+        ref = (key_hbm, val_hbm)[n]
         return remote(
             ref, kvown.at[slot, n], kv_send.at[n], kv_recv.at[slot, n], "seq", keeper
         )
@@ -169,13 +196,16 @@
         for n in range(2):
             kv_copy(n, place).start()
 
+    for copy in staged:
+        copy.wait()
+
     @pl.when(keeper == me)
     def _():
         kvown[place, 0] = key_ref[...]
         kvown[place, 1] = val_ref[...]
 
-    lane = lax.broadcasted_iota(jnp.int32, (some, hdim), 1)
-    hline = lax.broadcasted_iota(jnp.int32, (some, 1), 0)
+    def lane_of(p):
+        return lax.broadcasted_iota(jnp.int32, (sizes[p], hdim), 1)
 
     def lanes(h):
         return slice(h * hdim, (h + 1) * hdim)
@@ -185,7 +215,7 @@
 
     def p_copy(p, m):
         return remote(
-            sendb.at[m, p], recvb.at[me, p], p_send.at[p, m], p_recv.at[p, me], "seq", first + m
+            sendb[p].at[m], recvb[p].at[me], p_send.at[p, m], p_recv.at[p, me], "seq", first + m
         )
 
     @pl.when(is_live)
@@ -237,7 +267,7 @@
             )
 
         def message(p):
-            base = p * some * rows
+            base, some, lane = starts[p] * rows, sizes[p], lane_of(p)
             for m in range(mergers):
                 stat = None
                 for k in range(owned):
@@ -246,7 +276,7 @@
                         x = st2d[pl.ds(base + n, some, stride=rows), :]
                         here = (lane // 16 == k) & (lax.rem(lane, 4) // 2 == s)
                         stat = x if stat is None else jnp.where(here, x, stat)
-                        sendb[m, p, 2 * k + s] = o2d[
+                        sendb[p][m, 2 * k + s] = o2d[
                             pl.ds(base + n, some, stride=rows), :
                         ].astype(jnp.bfloat16)
                 high = stat.astype(jnp.bfloat16).astype(jnp.float32)
@@ -254,16 +284,17 @@
                 middle = rest.astype(jnp.bfloat16).astype(jnp.float32)
                 low = rest - middle
                 piece = lax.rem(lane, 16) // 4
-                sendb[m, p, 2 * owned] = jnp.where(
+                sendb[p][m, 2 * owned] = jnp.where(
                     piece == 0, high, jnp.where(piece == 1, middle, low)
                 ).astype(jnp.bfloat16)
 
+        half = heads // 2 if groups % 2 == 0 else heads
         for h in range(heads + 2 * LAG):
-            if h % some == 0 and h < heads:
-                for g in range(h // unit, (h + some) // unit):
+            if h < heads and h % half == 0:
+                for g in range(h // unit, (h + half) // unit):
                     k_copy(g).wait()
                     v_copy(g).wait()
-                if h + some == heads:
+                if h + half == heads:
                     for g in range(groups):
                         w_copy(g).start()
             if h < heads:
@@ -272,8 +303,8 @@
                 soften(h - LAG)
             if 0 <= h - 2 * LAG:
                 weigh(h - 2 * LAG)
-            if h - 2 * LAG >= 0 and (h - 2 * LAG + 1) % some == 0:
-                p = (h - 2 * LAG) // some
+            if h - 2 * LAG + 1 in starts[1:] + [heads]:
+                p = (starts[1:] + [heads]).index(h - 2 * LAG + 1)
                 message(p)
                 for m in range(mergers):
 
@@ -283,13 +314,13 @@
 
                     @pl.when(me == first + m)
                     def _():
-                        recvb[me, p] = sendb[m, p]
+                        recvb[p][me] = sendb[p][m]
 
     group = me - first
 
     def a_copy(p, to, n):
         return remote(
-            xin.at[group, p], xin.at[group, p], a_send.at[p, n], a_recv.at[p, group], "seq", to
+            xin[p].at[group], xin[p].at[group], a_send.at[p, n], a_recv.at[p, group], "seq", to
         )
 
     @pl.when(is_merger)
@@ -303,19 +334,20 @@
                     kv_copy(n, k).wait_recv()
 
         for k in range(owned):
-            parts = (qall.at[base + k], kvown.at[k, 0], kvown.at[k, 1])
-            for n, ref in enumerate(parts):
+            for n, ref in enumerate((qall.at[base + k], kvown.at[k, 0], kvown.at[k, 1])):
                 for h in range(heads):
                     own2d[k, n, 2 * h : 2 * h + 2, :] = ref[:, lanes(h)].astype(jnp.float32)
 
         def own_terms(k, p):
+            some, begin, lane = sizes[p], starts[p], lane_of(p)
+            hline = lax.broadcasted_iota(jnp.int32, (some, 1), 0)
             own = [
-                [own2d.at[k, n][pl.ds(2 * p * some + t, some, stride=2), :] for t in range(2)]
+                [own2d.at[k, n][pl.ds(2 * begin + t, some, stride=2), :] for t in range(2)]
                 for n in range(3)
             ]
             slope_col = jnp.zeros((some, 1), jnp.float32)
             for h in range(some):
-                slope_col = jnp.where(hline == h, slope_ref[p * some + h], slope_col)
+                slope_col = jnp.where(hline == h, slope_ref[begin + h], slope_col)
             e00 = jnp.sum(own[0][0] * own[1][0], axis=-1, keepdims=True) * scale
             e10 = jnp.sum(own[0][1] * own[1][0], axis=-1, keepdims=True) * scale - slope_col
             e11 = jnp.sum(own[0][1] * own[1][1], axis=-1, keepdims=True) * scale
@@ -328,15 +360,16 @@
             )
             return stat, [own[2][0], w10 * own[2][0] + w11 * own[2][1]]
 
-        own = [[own_terms(k, p) for k in range(owned)] for p in range(PARTS)]
+        own = [[own_terms(k, p) for k in range(owned)] for p in range(parts)]
 
         def merge(p):
+            some, lane = sizes[p], lane_of(p)
             stat = own[p][0][0]
             for k in range(1, owned):
                 stat = jnp.where(lane // 16 == k, own[p][k][0], stat)
             stats = [stat]
             for j in range(live):
-                x = recvb[j, p, 2 * owned].astype(jnp.float32)
+                x = recvb[p][j, 2 * owned].astype(jnp.float32)
                 x = x + pltpu.roll(x, hdim - 4, 1) + pltpu.roll(x, hdim - 8, 1)
                 stats.append(x)
             highest = functools.reduce(jnp.maximum, stats)
@@ -348,24 +381,24 @@
                     c = slice(16 * k + 2 * s, 16 * k + 2 * s + 1)
                     acc = factors[0][:, c] * own[p][k][1][s]
                     for j in range(live):
-                        acc += factors[j + 1][:, c] * recvb[j, p, 2 * k + s].astype(jnp.float32)
+                        acc += factors[j + 1][:, c] * recvb[p][j, 2 * k + s].astype(jnp.float32)
                     n = k // per * 2 * per + s * per + k % per
                     q2d[pl.ds(n * slot, some), :] = acc * inverse[:, c]
             for h in range(some):
-                xin[group, p, :, lanes(h)] = q2d[
+                xin[p][group, :, lanes(h)] = q2d[
                     pl.ds(h, 2 * owned, stride=slot), :
                 ].astype(jnp.bfloat16)
 
-        for p in range(PARTS):
+        for p in range(parts):
             for step in range(1, live):
                 source = to_live(step)
                 remote(
-                    sendb.at[0, p], recvb.at[source, p], p_send.at[p, 0], p_recv.at[p, source],
+                    sendb[p].at[0], recvb[p].at[source], p_send.at[p, 0], p_recv.at[p, source],
                     "seq", source,
                 ).wait_recv()
             merge(p)
             for n in range(1, n_seq):
-                a_copy(p, to_seq(n_seq - n), n - 1).start()
+                a_copy(p, other(n - 1), n - 1).start()
 
     for g in range(groups):
         w_copy(g).wait()
@@ -381,24 +414,24 @@
             to_head(step),
         )
 
-    for p in range(PARTS):
+    for p in range(parts):
         for m in range(mergers):
 
             @pl.when(me != first + m)
             def _():
-                here = xin.at[m, p]
+                here = xin[p].at[m]
                 remote(
                     here, here, a_send.at[p, 0], a_recv.at[p, m], "seq", first + m
                 ).wait_recv()
 
-        x = jnp.concatenate([xin[m, p] for m in range(mergers)], axis=0)
-        deep = slice(p * some * hdim, (p + 1) * some * hdim)
+        x = jnp.concatenate([xin[p][m] for m in range(mergers)], axis=0)
+        deep = slice(starts[p] * hdim, (starts[p] + sizes[p]) * hdim)
         for c in range(cols // tile):
             at = slice(c * tile, (c + 1) * tile)
             part = jnp.dot(x, wbuf[deep, at], preferred_element_type=jnp.float32)
             if p > 0:
                 part += sofar[:, at]
-            if p < PARTS - 1:
+            if p < parts - 1:
                 sofar[:, at] = part
                 continue
             for k in range(n_head):
@@ -424,7 +457,7 @@
 
             @pl.when(me != first + m)
             def _():
-                for p in range(PARTS):
+                for p in range(parts):
                     p_copy(p, m).wait_send()
 
     @pl.when(jnp.logical_not(is_live))
@@ -439,9 +472,9 @@
 
     @pl.when(is_merger)
     def _():
-        for p in range(PARTS):
+        for p in range(parts):
             for n in range(1, n_seq):
-                a_copy(p, to_seq(n_seq - n), n - 1).wait_send()
+                a_copy(p, other(n - 1), n - 1).wait_send()
 
     for step in range(1, n_head):
         for c in range(cols // tile):
@@ -473,24 +506,32 @@
     tile = cols
     rows = 2 * n_seq
     per = n_seq // n_head
-    some = heads // PARTS
-    slot = -(-some // 8) * 8
-    live, first, mergers = 3 * n_seq // 4, n_seq // 4, n_seq // 4
+    sizes = (heads * 3 // 7, heads * 2 // 7, heads * 2 // 7)
+    parts = len(sizes)
+    slot = -(-max(sizes) // 8) * 8
+    live, first, mergers = 3 * n_seq // 4, 0, n_head
     owned = n_seq // mergers
     assert n_seq % 4 == 0 and owned % per == 0 and 16 * owned <= hdim
-    assert heads % PARTS == 0
+    assert sum(sizes) == heads
     groups = heads // unit
     bf16, f32 = jnp.bfloat16, jnp.float32
     dma = pltpu.SemaphoreType.DMA
     vmem = pl.BlockSpec(memory_space=pltpu.VMEM)
-    smem = pl.BlockSpec(memory_space=pltpu.SMEM)
     hbm = pl.BlockSpec(memory_space=pl.ANY)
     return pl.pallas_call(
-        functools.partial(kernel, n_seq, n_head, heads, unit, tile, live, first, mergers),
+        functools.partial(kernel, n_seq, n_head, heads, unit, tile, live, first, mergers, sizes),
         out_shape=jax.ShapeDtypeStruct(residual.shape, residual.dtype),
-        in_specs=[vmem, vmem, vmem, smem, smem, smem, vmem, hbm, hbm, hbm],
+        in_specs=[hbm] * 10,
         out_specs=vmem,
         scratch_shapes=[
+            pltpu.VMEM((2, width), bf16),
+            pltpu.VMEM((2, width), bf16),
+            pltpu.VMEM((2, width), bf16),
+            pltpu.SMEM(seg_blocks.shape, jnp.int32),
+            pltpu.SMEM(request_row.shape, jnp.int32),
+            pltpu.SMEM(slopes.shape, f32),
+            pltpu.VMEM(residual.shape, bf16),
+            dma((7,)),
             pltpu.VMEM(cache_keys.shape, bf16),
             pltpu.VMEM(cache_values.shape, bf16),
             pltpu.VMEM(out_weight.shape, bf16),
@@ -504,9 +545,9 @@
             pltpu.VMEM((rows, tokens), f32),
             pltpu.VMEM((heads * rows, hdim), f32),
             pltpu.VMEM((heads * rows, hdim), f32),
-            pltpu.VMEM((mergers, PARTS, 2 * owned + 1, some, hdim), bf16),
-            pltpu.VMEM((live, PARTS, 2 * owned + 1, some, hdim), bf16),
-            pltpu.VMEM((mergers, PARTS, 2 * owned, some * hdim), bf16),
+            tuple(pltpu.VMEM((mergers, 2 * owned + 1, n, hdim), bf16) for n in sizes),
+            tuple(pltpu.VMEM((live, 2 * owned + 1, n, hdim), bf16) for n in sizes),
+            tuple(pltpu.VMEM((mergers, 2 * owned, n * hdim), bf16) for n in sizes),
             pltpu.VMEM((rows, cols), f32),
             pltpu.VMEM((n_head, 2 * per, cols), bf16),
             pltpu.VMEM((n_head - 1, 2 * per, cols), bf16),
@@ -517,10 +558,10 @@
             dma((n_seq,)),
             dma((2,)),
             dma((owned, 2)),
-            dma((PARTS, mergers)),
-            dma((PARTS, live)),
-            dma((PARTS, n_seq - 1)),
-            dma((PARTS, mergers)),
+            dma((parts, mergers)),
+            dma((parts, live)),
+            dma((parts, n_seq - 1)),
+            dma((parts, mergers)),
             dma((cols // tile, n_head - 1)),
             dma((cols // tile, n_head - 1)),
         ],

time: 29.6 us -> 26.9 us (0.909)
  Pallas kernels: 28 us -> 25.3 us
    pallas_call x1, Pallas kernels: 28 us -> 25.3 us  [body(): pl.pallas_call(functools.partial(kernel, n_seq, n_head, heads, unit, tile...]
where the time goes in v3:
time: 26.9 us; the launch traced here: 26.6 us
  Pallas kernels  25.3 us (94%)
  local copies, waits for them, and re-layouts  1.32 us (5%)
    pallas_call x1, Pallas kernels, body(): pl.pallas_call(functools.partial(kernel, n_seq, n_head, heads, unit, tile...  25.3 us
    unnamed x1, local copies, waits for them, and re-layouts  1.32 us

profile of v3, /device:TPU:0, one launch (start us, length us, event | category | flops | bytes accessed | tf_op | source)
XLA Modules:
  0.0 26.6 jit_solution(6675916215063757649)
XLA Ops:
  0.0 25.3 %shard_map.100 = bf16[2,2,1792]{2,1,0:T(2,128)(2,1)} custom-call(bf16[2,3584]{1,0:T(2,128)(2,1)} %bitcast.3, bf16[2,3584]{1,0:T(2,128)(2,1)} %bitcast.4, bf16[2,3584]{1,0:T(2,128)(2,1)} %bitcast.5, s32[8]{0:T(128)} %seg_hbm.1, s32[8]{0:T(128)} %row_hbm.1, f32[28]{0:T(128)} %slope_hbm.1, bf16[2,2,1792]{2,1,0:T(2,128)(2,1)} %res_hbm.1, ...), custom_call_target="tpu_custom_call" | custom-call | tf_op jit(solution)/shard_map/pallas_call | solution.py:521
  25.3 1.3 %copy.12 = bf16[2,2,1792]{2,1,0:T(2,128)(2,1)} copy(bf16[2,2,1792]{2,1,0:T(2,128)(2,1)} %shard_map.100) | data formatting | bytes 28672

commit v4 on v3

--- a/solution.py
+++ b/solution.py
@@ -44,6 +44,7 @@
     res_ref,
     i_sem,
     kbuf,
+    kturn,
     vbuf,
     wbuf,
     qall,
@@ -146,7 +147,6 @@
     def _():
         for g in range(groups):
             k_copy(g).start()
-            v_copy(g).start()
 
     barrier = pltpu.get_barrier_semaphore()
 
@@ -235,6 +235,13 @@
         dist[...] = jnp.where((token >= begin) & (token < end), gap, FAR)
         odd = lax.rem(lax.broadcasted_iota(jnp.int32, (rows, hdim), 1), 2) == 1
 
+        for g in range(groups):
+            k_copy(g).wait()
+            if g == 0:
+                for i in range(groups):
+                    v_copy(i).start()
+            for h in range(g * unit, (g + 1) * unit):
+                kturn[lanes(h), :] = kbuf[:, lanes(h)].T
         qall[me] = qry_ref[...]
         for step in range(1, n_seq):
             source = to_seq(step)
@@ -245,10 +252,9 @@
             qx[2 * r : 2 * r + 2, :] = qall[r].astype(jnp.float32)
 
         def scores(h):
-            dots = lax.dot_general(
+            dots = jnp.dot(
                 qx[:, lanes(h)].astype(jnp.bfloat16),
-                kbuf[:, lanes(h)],
-                (((1,), (1,)), ((), ())),
+                kturn[lanes(h), :],
                 preferred_element_type=jnp.float32,
             )
             sbuf[lines(h), :] = dots * scale - slope_ref[h] * dist[...]
@@ -288,20 +294,15 @@
                     piece == 0, high, jnp.where(piece == 1, middle, low)
                 ).astype(jnp.bfloat16)
 
-        half = heads // 2 if groups % 2 == 0 else heads
         for h in range(heads + 2 * LAG):
-            if h < heads and h % half == 0:
-                for g in range(h // unit, (h + half) // unit):
-                    k_copy(g).wait()
-                    v_copy(g).wait()
-                if h + half == heads:
-                    for g in range(groups):
-                        w_copy(g).start()
             if h < heads:
                 scores(h)
             if 0 <= h - LAG < heads:
                 soften(h - LAG)
             if 0 <= h - 2 * LAG:
+                if (h - 2 * LAG) % unit == 0:
+                    v_copy((h - 2 * LAG) // unit).wait()
+                    w_copy((h - 2 * LAG) // unit).start()
                 weigh(h - 2 * LAG)
             if h - 2 * LAG + 1 in starts[1:] + [heads]:
                 p = (starts[1:] + [heads]).index(h - 2 * LAG + 1)
@@ -533,6 +534,7 @@
             pltpu.VMEM(residual.shape, bf16),
             dma((7,)),
             pltpu.VMEM(cache_keys.shape, bf16),
+            pltpu.VMEM((width, tokens), bf16),
             pltpu.VMEM(cache_values.shape, bf16),
             pltpu.VMEM(out_weight.shape, bf16),
             pltpu.VMEM((n_seq, 2, width), bf16),

time: 26.9 us -> 26.1 us (0.970)
  Pallas kernels: 25.3 us -> 24.5 us
    pallas_call x1, Pallas kernels: 25.3 us -> 24.5 us  [body(): pl.pallas_call(functools.partial(kernel, n_seq, n_head, heads, unit, tile...]
where the time goes in v4:
time: 26.1 us; the launch traced here: 25.9 us
  Pallas kernels  24.5 us (94%)
  local copies, waits for them, and re-layouts  1.32 us (5%)
    pallas_call x1, Pallas kernels, body(): pl.pallas_call(functools.partial(kernel, n_seq, n_head, heads, unit, tile...  24.5 us
    unnamed x1, local copies, waits for them, and re-layouts  1.32 us

profile of v4, /device:TPU:0, one launch (start us, length us, event | category | flops | bytes accessed | tf_op | source)
XLA Modules:
  0.0 25.9 jit_solution(4138257806922562010)
XLA Ops:
  0.0 24.5 %shard_map.100 = bf16[2,2,1792]{2,1,0:T(2,128)(2,1)} custom-call(bf16[2,3584]{1,0:T(2,128)(2,1)} %bitcast.3, bf16[2,3584]{1,0:T(2,128)(2,1)} %bitcast.4, bf16[2,3584]{1,0:T(2,128)(2,1)} %bitcast.5, s32[8]{0:T(128)} %seg_hbm.1, s32[8]{0:T(128)} %row_hbm.1, f32[28]{0:T(128)} %slope_hbm.1, bf16[2,2,1792]{2,1,0:T(2,128)(2,1)} %res_hbm.1, ...), custom_call_target="tpu_custom_call" | custom-call | tf_op jit(solution)/shard_map/pallas_call | solution.py:522
  24.5 1.3 %copy.12 = bf16[2,2,1792]{2,1,0:T(2,128)(2,1)} copy(bf16[2,2,1792]{2,1,0:T(2,128)(2,1)} %shard_map.100) | data formatting | bytes 28672

commit v5 on v4

--- a/solution.py
+++ b/solution.py
@@ -272,27 +272,26 @@
                 pbuf[lines(h), :], vbuf[:, lanes(h)], preferred_element_type=jnp.float32
             )
 
-        def message(p):
+        def message(p, m):
             base, some, lane = starts[p] * rows, sizes[p], lane_of(p)
-            for m in range(mergers):
-                stat = None
-                for k in range(owned):
-                    for s in range(2):
-                        n = 2 * (m * owned + k) + s
-                        x = st2d[pl.ds(base + n, some, stride=rows), :]
-                        here = (lane // 16 == k) & (lax.rem(lane, 4) // 2 == s)
-                        stat = x if stat is None else jnp.where(here, x, stat)
-                        sendb[p][m, 2 * k + s] = o2d[
-                            pl.ds(base + n, some, stride=rows), :
-                        ].astype(jnp.bfloat16)
-                high = stat.astype(jnp.bfloat16).astype(jnp.float32)
-                rest = stat - high
-                middle = rest.astype(jnp.bfloat16).astype(jnp.float32)
-                low = rest - middle
-                piece = lax.rem(lane, 16) // 4
-                sendb[p][m, 2 * owned] = jnp.where(
-                    piece == 0, high, jnp.where(piece == 1, middle, low)
-                ).astype(jnp.bfloat16)
+            stat = None
+            for k in range(owned):
+                for s in range(2):
+                    n = 2 * (m * owned + k) + s
+                    x = st2d[pl.ds(base + n, some, stride=rows), :]
+                    here = (lane // 16 == k) & (lax.rem(lane, 4) // 2 == s)
+                    stat = x if stat is None else jnp.where(here, x, stat)
+                    sendb[p][m, 2 * k + s] = o2d[
+                        pl.ds(base + n, some, stride=rows), :
+                    ].astype(jnp.bfloat16)
+            high = stat.astype(jnp.bfloat16).astype(jnp.float32)
+            rest = stat - high
+            middle = rest.astype(jnp.bfloat16).astype(jnp.float32)
+            low = rest - middle
+            piece = lax.rem(lane, 16) // 4
+            sendb[p][m, 2 * owned] = jnp.where(
+                piece == 0, high, jnp.where(piece == 1, middle, low)
+            ).astype(jnp.bfloat16)
 
         for h in range(heads + 2 * LAG):
             if h < heads:
@@ -306,8 +305,8 @@
                 weigh(h - 2 * LAG)
             if h - 2 * LAG + 1 in starts[1:] + [heads]:
                 p = (starts[1:] + [heads]).index(h - 2 * LAG + 1)
-                message(p)
-                for m in range(mergers):
+                for m in reversed(range(mergers)):
+                    message(p, m)
 
                     @pl.when(me != first + m)
                     def _():
@@ -521,7 +520,7 @@
     hbm = pl.BlockSpec(memory_space=pl.ANY)
     return pl.pallas_call(
         functools.partial(kernel, n_seq, n_head, heads, unit, tile, live, first, mergers, sizes),
-        out_shape=jax.ShapeDtypeStruct(residual.shape, residual.dtype),
+        out_shape=pltpu.VMEM(residual.shape, residual.dtype),
         in_specs=[hbm] * 10,
         out_specs=vmem,
         scratch_shapes=[

time: 26.1 us -> 24.4 us (0.935)
  Pallas kernels: 24.5 us -> 23.7 us
  local copies, waits for them, and re-layouts: 1.32 us -> 0.6 us
    pallas_call x1, Pallas kernels: 24.5 us -> 23.7 us  [body(): pl.pallas_call(functools.partial(kernel, n_seq, n_head, heads, unit, tile...]
    unnamed x1, local copies, waits for them, and re-layouts: 1.32 us -> 0.6 us
where the time goes in v5:
time: 24.4 us; the launch traced here: 24.3 us
  Pallas kernels  23.7 us (97%)
  local copies, waits for them, and re-layouts  0.6 us (2%)
    pallas_call x1, Pallas kernels, body(): pl.pallas_call(functools.partial(kernel, n_seq, n_head, heads, unit, tile...  23.7 us
    unnamed x1, local copies, waits for them, and re-layouts  0.6 us

profile of v5, /device:TPU:0, one launch (start us, length us, event | category | flops | bytes accessed | tf_op | source)
XLA Modules:
  0.0 24.3 jit_solution(586654591455032514)
XLA Ops:
  0.0 23.7 %shard_map.100 = bf16[2,2,1792]{2,1,0:T(2,128)(2,1)S(1)} custom-call(bf16[2,3584]{1,0:T(2,128)(2,1)} %bitcast.3, bf16[2,3584]{1,0:T(2,128)(2,1)} %bitcast.4, bf16[2,3584]{1,0:T(2,128)(2,1)} %bitcast.5, s32[8]{0:T(128)} %seg_hbm.1, s32[8]{0:T(128)} %row_hbm.1, f32[28]{0:T(128)} %slope_hbm.1, bf16[2,2,1792]{2,1,0:T(2,128)(2,1)} %res_hbm.1, ...), custom_call_target="tpu_custom_call" | custom-call | tf_op jit(solution)/shard_map/pallas_call | solution.py:521
  23.7 0.6 %copy.12 = bf16[2,2,1792]{2,1,0:T(2,128)(2,1)} copy(bf16[2,2,1792]{2,1,0:T(2,128)(2,1)S(1)} %shard_map.100) | data formatting | bytes 28672

commit v6 on v5

--- a/solution.py
+++ b/solution.py
@@ -439,6 +439,33 @@
             for step in range(1, n_head):
                 h_copy(c, step).start()
 
+    @pl.when(is_live)
+    def _():
+        for step in range(1, live):
+            q_copy(step - 1, to_live(step)).wait_send()
+        for m in range(mergers):
+
+            @pl.when(me != first + m)
+            def _():
+                for p in range(parts):
+                    p_copy(p, m).wait_send()
+
+    @pl.when(jnp.logical_not(is_live))
+    def _():
+        for d in range(live):
+            q_copy(d, d).wait_send()
+
+    @pl.when(keeper != me)
+    def _():
+        for n in range(2):
+            kv_copy(n, place).wait_send()
+
+    @pl.when(is_merger)
+    def _():
+        for p in range(parts):
+            for n in range(1, n_seq):
+                a_copy(p, other(n - 1), n - 1).wait_send()
+
     summed = shares[mine].astype(jnp.float32)
     for step in range(1, n_head):
         for c in range(cols // tile):
@@ -448,33 +475,6 @@
         out_ref[s] = (
             res_ref[s].astype(jnp.float32) + summed[s * per : (s + 1) * per]
         ).astype(jnp.bfloat16)
-
-    @pl.when(is_live)
-    def _():
-        for step in range(1, live):
-            q_copy(step - 1, to_live(step)).wait_send()
-        for m in range(mergers):
-
-            @pl.when(me != first + m)
-            def _():
-                for p in range(parts):
-                    p_copy(p, m).wait_send()
-
-    @pl.when(jnp.logical_not(is_live))
-    def _():
-        for d in range(live):
-            q_copy(d, d).wait_send()
-
-    @pl.when(keeper != me)
-    def _():
-        for n in range(2):
-            kv_copy(n, place).wait_send()
-
-    @pl.when(is_merger)
-    def _():
-        for p in range(parts):
-            for n in range(1, n_seq):
-                a_copy(p, other(n - 1), n - 1).wait_send()
 
     for step in range(1, n_head):
         for c in range(cols // tile):

time: 24.4 us -> 24.4 us (level)
  no operation moved by 1% of the time
where the time goes in v6:
time: 24.4 us; the launch traced here: 24.2 us
  Pallas kernels  23.6 us (97%)
  local copies, waits for them, and re-layouts  0.6 us (2%)
    pallas_call x1, Pallas kernels, body(): pl.pallas_call(functools.partial(kernel, n_seq, n_head, heads, unit, tile...  23.6 us
    unnamed x1, local copies, waits for them, and re-layouts  0.6 us

profile of v6, /device:TPU:0, one launch (start us, length us, event | category | flops | bytes accessed | tf_op | source)
XLA Modules:
  0.0 24.2 jit_solution(1289797162080567665)
XLA Ops:
  0.0 23.6 %shard_map.100 = bf16[2,2,1792]{2,1,0:T(2,128)(2,1)S(1)} custom-call(bf16[2,3584]{1,0:T(2,128)(2,1)} %bitcast.3, bf16[2,3584]{1,0:T(2,128)(2,1)} %bitcast.4, bf16[2,3584]{1,0:T(2,128)(2,1)} %bitcast.5, s32[8]{0:T(128)} %seg_hbm.1, s32[8]{0:T(128)} %row_hbm.1, f32[28]{0:T(128)} %slope_hbm.1, bf16[2,2,1792]{2,1,0:T(2,128)(2,1)} %res_hbm.1, ...), custom_call_target="tpu_custom_call" | custom-call | tf_op jit(solution)/shard_map/pallas_call | solution.py:521
  23.6 0.6 %copy.12 = bf16[2,2,1792]{2,1,0:T(2,128)(2,1)} copy(bf16[2,2,1792]{2,1,0:T(2,128)(2,1)S(1)} %shard_map.100) | data formatting | bytes 28672

commit v7 on v6

--- a/solution.py
+++ b/solution.py
@@ -308,13 +308,22 @@
                 for m in reversed(range(mergers)):
                     message(p, m)
 
-                    @pl.when(me != first + m)
-                    def _():
+                @pl.when(jnp.logical_not(is_merger))
+                def _():
+                    for m in reversed(range(mergers)):
                         p_copy(p, m).start()
 
-                    @pl.when(me == first + m)
-                    def _():
-                        recvb[p][me] = sendb[p][m]
+                @pl.when(is_merger)
+                def _():
+                    for m in reversed(range(mergers)):
+
+                        @pl.when(me != first + m)
+                        def _():
+                            p_copy(p, m).start()
+
+                        @pl.when(me == first + m)
+                        def _():
+                            recvb[p][me] = sendb[p][m]
 
     group = me - first
 

time: 24.4 us -> 24.4 us (level)
  no operation moved by 1% of the time
where the time goes in v7:
time: 24.4 us; the launch traced here: 24.2 us
  Pallas kernels  23.6 us (97%)
  local copies, waits for them, and re-layouts  0.6 us (2%)
    pallas_call x1, Pallas kernels, body(): pl.pallas_call(functools.partial(kernel, n_seq, n_head, heads, unit, tile...  23.6 us
    unnamed x1, local copies, waits for them, and re-layouts  0.6 us

profile of v7, /device:TPU:0, one launch (start us, length us, event | category | flops | bytes accessed | tf_op | source)
XLA Modules:
  0.0 24.2 jit_solution(4904149940537420999)
XLA Ops:
  0.0 23.6 %shard_map.100 = bf16[2,2,1792]{2,1,0:T(2,128)(2,1)S(1)} custom-call(bf16[2,3584]{1,0:T(2,128)(2,1)} %bitcast.3, bf16[2,3584]{1,0:T(2,128)(2,1)} %bitcast.4, bf16[2,3584]{1,0:T(2,128)(2,1)} %bitcast.5, s32[8]{0:T(128)} %seg_hbm.1, s32[8]{0:T(128)} %row_hbm.1, f32[28]{0:T(128)} %slope_hbm.1, bf16[2,2,1792]{2,1,0:T(2,128)(2,1)} %res_hbm.1, ...), custom_call_target="tpu_custom_call" | custom-call | tf_op jit(solution)/shard_map/pallas_call | solution.py:530
  23.6 0.6 %copy.12 = bf16[2,2,1792]{2,1,0:T(2,128)(2,1)} copy(bf16[2,2,1792]{2,1,0:T(2,128)(2,1)S(1)} %shard_map.100) | data formatting | bytes 28672
